TPU v7x, 32 devices: a whole 2x2x4 slice. The times are simulated.
32 devices in a mesh: parts: 2 (over y), seq: 4 (over x, core), mp: 4 (over z).
Axes of the slice: x: 2, y: 2, z: 4, core: 2. Of those that a mesh axis runs over, the one named last changes fastest.
Arguments:
- tokens: bfloat16 [4096, 8192], P(('parts', 'seq'), 'mp'), parts along dimension 0, may hold values from -6 to 6
- w_in: bfloat16 [3, 8192, 512], P(None, 'seq', 'mp'), may hold values from -0.0625 to 0.0625
- short_filter: float32 [3, 3, 512], P(None, None, 'mp'), may hold values from -3 to 3
- long_filter: float32 [32, 128], P('mp'), may hold values from -0.5 to 0.5
- skip: float32 [512], P('mp'), may hold values from -4 to 4
Outputs:
- mixed: bfloat16 [4096, 512], P(('parts', 'seq'), 'mp'), parts along dimension 0
There are 2 independent parts, one for each index of `parts`. A program takes and returns all parts, laid end to end along the dimension named above; an argument that names none is the same for every part. Nothing has to cross between parts.
All inputs are finite; a program needn't handle non-finite values.
Results may differ from a plain program's by a relative error of at most 0.0081.
Values may be sent and summed in bfloat16 or wider, within the bound.
A program may use at most 64 MiB of HBM per device.

v0:
```python
import jax
import jax.numpy as jnp
from jax import lax
from jax.sharding import PartitionSpec as P

FLT = 128
GRP = 16


def passed_along(block, axis, distance):
    devices = range(lax.axis_size(axis))
    route = [(i - distance, i) for i in devices if i - distance in devices]
    return lax.ppermute(block, axis, route)


def shards(tokens, w_in, short_filter, long_filter, skip):
    rows = tokens.shape[0]
    width = w_in.shape[2]
    groups = long_filter.shape[0]
    full_rows = lax.all_gather(tokens, "mp", axis=1, tiled=True)
    fullf = full_rows.astype(jnp.float32)
    meansq = jnp.mean(fullf * fullf, axis=1, keepdims=True)
    normed = (fullf * lax.rsqrt(meansq + 1e-06)).astype(jnp.bfloat16)
    proj = jnp.einsum(
        "td,pdc->tpc",
        normed,
        lax.all_gather(w_in, "seq", axis=1, tiled=True),
        preferred_element_type=jnp.float32,
    )
    proj = proj.astype(jnp.bfloat16)
    margin = FLT + 2
    tail = passed_along(proj[rows - margin :], "seq", 1)
    extended = jnp.concatenate([tail, proj], axis=0).astype(jnp.float32)
    length = FLT + rows
    sharp = jnp.zeros((length, 3, width), jnp.float32)
    for j in range(3):
        sharp = sharp + short_filter[:, j, :][None] * extended[2 - j : 2 - j + length]
    gated = sharp[:, 1] * sharp[:, 2]
    nblock = rows // FLT
    pieces = gated.reshape(nblock + 1, FLT, width)
    windows = jnp.concatenate([pieces[:-1], pieces[1:]], axis=1).reshape(
        nblock, 2 * FLT, groups, GRP
    )
    lead = jnp.zeros((groups, 1), jnp.float32)
    trail = jnp.zeros((groups, FLT), jnp.float32)
    table = jnp.concatenate([lead, long_filter[:, ::-1], trail], axis=1)
    toeplitz = jnp.tile(table, (1, FLT))[:, : FLT * 2 * FLT].reshape(groups, FLT, 2 * FLT)
    conv = jnp.einsum("gts,bsgk->btgk", toeplitz, windows, precision=lax.Precision.HIGHEST)
    filtered = conv.reshape(rows, width) + skip[None, :] * gated[FLT:]
    return (sharp[FLT:, 0] * filtered).astype(jnp.bfloat16)


def solution(mesh):
    return jax.shard_map(
        shards,
        mesh=mesh,
        in_specs=(
            P(("parts", "seq"), "mp"),
            P(None, "seq", "mp"),
            P(None, None, "mp"),
            P("mp", None),
            P("mp"),
        ),
        out_specs=P(("parts", "seq"), "mp"),
        check_vma=False,
    )
```

profile of v0, /device:TPU:1, one launch (start us, length us, event | category | flops | bytes accessed | tf_op | source)
XLA Modules:
  0.0 231.0 jit_solution(282545609042899873)
XLA Ops:
  6.5 0.7 all-gather.3.cloned.1.call-update
  7.3 0.7 all-gather.5.cloned.1.call-update
  8.0 0.8 rev.3
  8.8 0.1 pad.2.clone
  8.8 0.8 fusion.20
  9.7 0.1 maximum_maximum_fusion
  9.7 151.1 %all-gather.3.cloned.1.call-done = bf16[512,8192]{1,0:T(8,128)(2,1)} async-done(((bf16[512,2048]{1,0:T(8,128)(2,1)}), bf16[512,8192]{1,0:T(8,128)(2,1)}) %all-gather.3.cloned.1.call-update) | async-done | bytes 8388624 | tf_op jit(solution)/shard_map/all_gather | solution.py:20
  160.8 5.1 %fusion = f32[512]{0:T(512)S(1)} fusion(bf16[512,8192]{1,0:T(8,128)(2,1)} %all-gather.3.cloned.1.call-done), kind=kLoop, calls=%fused_computation.2 | loop fusion | flops 12582400 | bytes 8390656 | tf_op jit(solution)/shard_map/reduce_sum | solution.py:22
  165.9 41.3 %all-gather.5.cloned.1.call-done = bf16[3,8192,128]{2,1,0:T(8,128)(2,1)} async-done(((bf16[3,2048,128]{2,1,0:T(8,128)(2,1)}), bf16[3,8192,128]{2,1,0:T(8,128)(2,1)}) %all-gather.5.cloned.1.call-update) | async-done | bytes 6291472 | tf_op jit(solution)/shard_map/all_gather | solution.py:27
  207.2 9.7 %fusion.6 = bf16[512,3,128]{2,0,1:T(8,128)(2,1)S(1)} fusion(bf16[3,8192,128]{2,1,0:T(8,128)(2,1)} %all-gather.5.cloned.1.call-done, bf16[512,8192]{1,0:T(8,128)(2,1)} %all-gather.3.cloned.1.call-done, f32[512]{0:T(512)S(1)} %add_rsqrt_fusion), kind=kOutput, calls=%fused_computation.7 | convolution fusion | flops 3234004992 | bytes 15075328 | tf_op jit(solution)/shard_map/td,pdc->tpc/dot_general | solution.py:24
  216.9 2.1 collective-permute-start
  219.0 0.1 tile.4
  219.2 0.7 tile.10
  220.0 0.7 collective-permute-done
  220.7 0.1 maximum_convert_fusion
  220.8 0.3 fusion.10
  221.2 0.1 copy.9
  221.3 0.1 concatenate.15
  221.4 0.1 copy.10
  221.6 0.1 concatenate.16
  221.7 1.5 convolution_bitcast_fusion
  223.2 0.1 copy.13
  223.3 0.1 copy.14
  223.4 0.7 fusion.16
  (16 shorter events, 0.3 us)
Async XLA Ops:
  6.5 154.2 %all-gather.3.cloned.1.call-start = ((), (), s32[]{:S(2)}) async-start(), calls=%async_computation | async-start | bytes 10485760 | tf_op jit(solution)/shard_map/all_gather | solution.py:20
  7.3 199.9 %all-gather.5.cloned.1.call-start = ((), (), s32[]{:S(2)}) async-start(), calls=%async_computation.1 | async-start | bytes 7864320 | tf_op jit(solution)/shard_map/all_gather | solution.py:27
  216.9 3.8 %collective-permute-start = (bf16[130,3,128]{2,0,1:T(8,128)(2,1)S(1)}, bf16[130,3,128]{2,0,1:T(8,128)(2,1)S(1)}, u32[]{:S(2)}, u32[]{:S(2)}) collective-permute-start(bf16[130,3,128]{2,0,1:T(8,128)(2,1)S(1)} %slice.60), channel_id=1, source_target_pairs={{0,4},{4,8},{8,12},{1,5},{5,9},{9,13},{2,6},{6,10},{10,14},{3,7},{... | collective-permute-start | bytes 299528 | tf_op jit(solution)/shard_map/ppermute | solution.py:13
  219.9 3.5 %copy-start = (f32[128]{0:T(128)S(1)}, f32[128]{0:T(128)}, u32[]{:S(2)}) copy-start(f32[128]{0:T(128)} %param.9) | copy-start | bytes 1540
Sparse Core Ops, SparseCore 0:
  8.9 151.8 all-gather.2
  162.3 44.7 all-gather.4
where the time goes:
time: 231 us
  waiting for transfers between devices  194 us (84%)
  between operations  13.6 us (6%)
  matrix products  11.1 us (5%)
  other arithmetic  6.3 us (3%)
  local copies, waits for them, and re-layouts  3.36 us (1%)
    all_gather x1, waiting for transfers between devices, shards(): full_rows = lax.all_gather(tokens, 'mp', axis=1, tiled=True)  151 us
    all_gather x1, waiting for transfers between devices, shards(): lax.all_gather(w_in, 'seq', axis=1, tiled=True)  41.3 us
    dot_general x1, matrix products, shards(): jnp.einsum('td,pdc->tpc', normed, lax.all_gather(w_in, 'seq', axis=1, til...  9.69 us
    reduce_sum x1, other arithmetic, shards(): meansq = jnp.mean(fullf * fullf, axis=1, keepdims=True)  5.1 us
  transfers between devices with their start and end apart: 3, of which 3 were waited for; matrix products, arithmetic and copies ran while one was open for 3% of the time, Pallas kernels for 0%

commit v1 on v0

--- a/solution.py
+++ b/solution.py
@@ -1,6 +1,10 @@
+import functools
+
 import jax
 import jax.numpy as jnp
 from jax import lax
+from jax.experimental import pallas as pl
+from jax.experimental.pallas import tpu as pltpu
 from jax.sharding import PartitionSpec as P
 
 FLT = 128
@@ -13,24 +17,231 @@
     return lax.ppermute(block, axis, route)
 
 
+def project(Y, S, M, x_ref, w_ref, out_ref, wbuf, pbuf, rbuf, pself, ssbuf,
+            send1, send_a, recv_a, send_b, recv_b, send_p, recv_p, send_s, recv_s):
+    X, R = S // 2, M // S
+    T, F = x_ref.shape
+    part_rows = F // Y
+    y, s, m = lax.axis_index("parts"), lax.axis_index("seq"), lax.axis_index("mp")
+    x, core = s // 2, s % 2
+
+    def at(y_, s_, m_):
+        return {"parts": y_, "seq": s_, "mp": m_}
+
+    mq = m % S
+    relay = 2 * (mq % X) + mq // X
+    family = x + core * X
+
+    def is_self(r):
+        return jnp.logical_and(relay == s, R * s + r == m)
+
+    def source_is_self(r2):
+        return jnp.logical_and(m // R == s, family + S * r2 == m)
+
+    def chunk(y_, x_, core_, r2):
+        c = x_ + core_ * X + S * r2
+        return wbuf.at[c, :, pl.ds(pl.multiple_of(y_ * part_rows, part_rows), part_rows), :]
+
+    def arrived(ref, sem):
+        pltpu.make_async_copy(ref, ref, sem).wait()
+
+    others = [(dy, dx) for dx in range(X) for dy in range(Y) if dy or dx]
+
+    def other(dy, dx):
+        return (y + dy) % Y, (x + dx) % X
+
+    barrier = pltpu.get_barrier_semaphore()
+
+    def greet(dev):
+        pl.semaphore_signal(barrier, inc=1, device_id=dev, device_id_type=pl.DeviceIdType.MESH)
+
+    for r in range(R):
+        @pl.when(jnp.logical_not(is_self(r)))
+        def _(r=r):
+            greet(at(y, relay, R * s + r))
+
+        @pl.when(jnp.logical_not(source_is_self(r)))
+        def _(r=r):
+            greet(at(y, m // R, family + S * r))
+    for dy, dx in others:
+        yo, xo = other(dy, dx)
+        greet(at(yo, 2 * xo + core, m))
+    greet(at(y, 2 * x + 1 - core, m))
+    for k in range(1, M):
+        greet(at(y, s, (m + k) % M))
+    peers = len(others) + 1 + M - 1 + 2 * R
+    for r in range(R):
+        peers = peers - is_self(r).astype(jnp.int32) - source_is_self(r).astype(jnp.int32)
+    pl.semaphore_wait(barrier, peers)
+
+    def first(r):
+        rows = pl.ds(pl.multiple_of(r * F + y * part_rows, part_rows), part_rows)
+        dst = wbuf.at[m, :, pl.ds(pl.multiple_of(y * part_rows, part_rows), part_rows), :]
+        rx, rc = relay // 2, relay % 2
+        sem = recv_a.at[y, rx, m // S]
+        return w_ref.at[:, rows, :], dst, sem, rx, rc
+
+    for r in range(R):
+        src, dst, sem, _, _ = first(r)
+
+        @pl.when(is_self(r))
+        def _(src=src, dst=dst, sem=sem):
+            pltpu.make_async_copy(src, dst, sem).start()
+
+        @pl.when(jnp.logical_not(is_self(r)))
+        def _(src=src, dst=dst, sem=sem, r=r):
+            pltpu.make_async_remote_copy(
+                src_ref=src, dst_ref=dst, send_sem=send1.at[r], recv_sem=sem,
+                device_id=at(y, relay, R * s + r), device_id_type=pl.DeviceIdType.MESH,
+            ).start()
+
+    tile = min(T, 128)
+
+    for i in range(T // tile):
+        xf = x_ref[i * tile:(i + 1) * tile, :].astype(jnp.float32)
+        ss = jnp.sum(xf * xf, axis=1, keepdims=True)
+        ssbuf[m, :, i * tile:(i + 1) * tile] = jnp.transpose(jnp.broadcast_to(ss, (tile, 128)))[:8]
+
+    def share_squares(k):
+        return pltpu.make_async_remote_copy(
+            src_ref=ssbuf.at[m], dst_ref=ssbuf.at[m], send_sem=send_s.at[k], recv_sem=recv_s.at[m],
+            device_id=at(y, s, (m + k) % M), device_id_type=pl.DeviceIdType.MESH)
+
+    for k in range(1, M):
+        share_squares(k).start()
+
+    def hand(dy, dx, r2):
+        yo, xo = other(dy, dx)
+        ref = chunk(y, x, core, r2)
+        return pltpu.make_async_remote_copy(
+            src_ref=ref, dst_ref=ref, send_sem=send_a.at[dy, dx, r2], recv_sem=recv_a.at[y, x, r2],
+            device_id=at(yo, 2 * xo + core, m), device_id_type=pl.DeviceIdType.MESH)
+
+    def pass_on(dy, dx, r2):
+        yo, xo = other(dy, dx)
+        ref = chunk(yo, xo, core, r2)
+        return pltpu.make_async_remote_copy(
+            src_ref=ref, dst_ref=ref, send_sem=send_b.at[yo, xo, r2], recv_sem=recv_b.at[yo, xo, r2],
+            device_id=at(y, 2 * x + 1 - core, m), device_id_type=pl.DeviceIdType.MESH)
+
+    def send_partial(c):
+        return pltpu.make_async_remote_copy(
+            src_ref=pbuf.at[c], dst_ref=rbuf.at[m], send_sem=send_p.at[c], recv_sem=recv_p.at[m],
+            device_id=at(y, s, c), device_id_type=pl.DeviceIdType.MESH)
+
+    def multiply(c):
+        w = jnp.concatenate([wbuf[c, p] for p in range(3)], axis=1)
+        part = jnp.dot(x_ref[...], w, preferred_element_type=jnp.float32)
+
+        @pl.when(c == m)
+        def _():
+            pself[...] = part
+
+        @pl.when(c != m)
+        def _():
+            pbuf[c] = part.astype(pbuf.dtype)
+            send_partial(c).start()
+
+    for r2 in range(R):
+        arrived(chunk(y, x, core, r2), recv_a.at[y, x, r2])
+        for dy, dx in others:
+            hand(dy, dx, r2).start()
+        pass_on(0, 0, r2).start()
+
+    def take(dy, dx):
+        for r2 in range(R):
+            yo, xo = other(dy, dx)
+            arrived(chunk(yo, xo, core, r2), recv_a.at[yo, xo, r2])
+            pass_on(dy, dx, r2).start()
+
+    def work(dx, mine):
+        xo = (x + dx) % X
+        core_ = core if mine else 1 - core
+
+        def one(r2, carry):
+            if not mine:
+                for dy in range(Y):
+                    yo = (y + dy) % Y
+                    arrived(chunk(yo, xo, core_, r2), recv_b.at[yo, xo, r2])
+            multiply(xo + core_ * X + S * r2)
+            return carry
+        lax.fori_loop(0, R, one, 0)
+
+    for dx in range(X):
+        for dy in range(Y):
+            if dy or dx:
+                take(dy, dx)
+        work(dx, True)
+        work(dx, False)
+
+    for k in range(1, M):
+        c = (m + k) % M
+        arrived(ssbuf.at[c], recv_s.at[c])
+    total = ssbuf[0]
+    for c in range(1, M):
+        total = total + ssbuf[c]
+    inv = lax.rsqrt(total / (F * M) + 1e-06)
+    for k in range(1, M):
+        c = (m + k) % M
+        arrived(rbuf.at[c], recv_p.at[c])
+    for i in range(T // tile):
+        rows = slice(i * tile, (i + 1) * tile)
+
+        def add(k, acc):
+            return acc + rbuf[(m + k) % M, rows, :].astype(jnp.float32)
+        acc = lax.fori_loop(1, M, add, pself[rows, :])
+        scale = jnp.transpose(jnp.broadcast_to(inv[0:1, rows], (128, tile)))
+        out_ref[rows, :] = acc * jnp.concatenate([scale] * 3, axis=1)
+
+    for r in range(R):
+        @pl.when(jnp.logical_not(is_self(r)))
+        def _(r=r):
+            src = first(r)[0]
+            arrived(src, send1.at[r])
+    for k in range(1, M):
+        share_squares(k).wait_send()
+        send_partial((m + k) % M).wait_send()
+    for r2 in range(R):
+        for dy in range(Y):
+            for dx in range(X):
+                if dy or dx:
+                    hand(dy, dx, r2).wait_send()
+                pass_on(dy, dx, r2).wait_send()
+
+
+def projected(tokens, w_in):
+    Y, S, M = (lax.axis_size(a) for a in ("parts", "seq", "mp"))
+    T, F = tokens.shape
+    X, R = S // 2, M // S
+    W = 3 * w_in.shape[2]
+    dma = pltpu.SemaphoreType.DMA
+    return pl.pallas_call(
+        functools.partial(project, Y, S, M),
+        out_shape=jax.ShapeDtypeStruct((T, W), jnp.float32),
+        in_specs=[pl.BlockSpec(memory_space=pltpu.VMEM), pl.BlockSpec(memory_space=pl.ANY)],
+        out_specs=pl.BlockSpec(memory_space=pltpu.VMEM),
+        scratch_shapes=[
+            pltpu.VMEM((M, 3, F, w_in.shape[2]), jnp.bfloat16),
+            pltpu.VMEM((M, T, W), jnp.bfloat16),
+            pltpu.VMEM((M, T, W), jnp.bfloat16),
+            pltpu.VMEM((T, W), jnp.float32),
+            pltpu.VMEM((M, 8, T), jnp.float32),
+            dma((R,)), dma((Y, X, R)), dma((Y, X, R)), dma((Y, X, R)), dma((Y, X, R)),
+            dma((M,)), dma((M,)), dma((M,)), dma((M,)),
+        ],
+        compiler_params=pltpu.CompilerParams(
+            collective_id=0, has_side_effects=True, vmem_limit_bytes=56 * 2**20),
+    )(tokens, w_in)
+
+
 def shards(tokens, w_in, short_filter, long_filter, skip):
     rows = tokens.shape[0]
     width = w_in.shape[2]
     groups = long_filter.shape[0]
-    full_rows = lax.all_gather(tokens, "mp", axis=1, tiled=True)
-    fullf = full_rows.astype(jnp.float32)
-    meansq = jnp.mean(fullf * fullf, axis=1, keepdims=True)
-    normed = (fullf * lax.rsqrt(meansq + 1e-06)).astype(jnp.bfloat16)
-    proj = jnp.einsum(
-        "td,pdc->tpc",
-        normed,
-        lax.all_gather(w_in, "seq", axis=1, tiled=True),
-        preferred_element_type=jnp.float32,
-    )
-    proj = proj.astype(jnp.bfloat16)
+    proj = projected(tokens, w_in).reshape(rows, 3, width)
     margin = FLT + 2
-    tail = passed_along(proj[rows - margin :], "seq", 1)
-    extended = jnp.concatenate([tail, proj], axis=0).astype(jnp.float32)
+    tail = passed_along(proj[rows - margin :].astype(jnp.bfloat16), "seq", 1).astype(jnp.float32)
+    extended = jnp.concatenate([tail, proj], axis=0)
     length = FLT + rows
     sharp = jnp.zeros((length, 3, width), jnp.float32)
     for j in range(3):

time: 231 us -> 125 us (0.54)
  waiting for transfers between devices: 194 us -> 0.01 us
  Pallas kernels: 0 us -> 96.4 us
  starting transfers between devices: 2.15 us -> 17.4 us
  between operations: 13.6 us -> 0.2 us
  matrix products: 11.1 us -> 1.45 us
  other arithmetic: 6.3 us -> 2.07 us
  local copies, waits for them, and re-layouts: 3.36 us -> 7.57 us
    all_gather x2 -> x0, waiting for transfers between devices: 192 us -> none  [the longest x1 151 us: shards(): full_rows = lax.all_gather(tokens, 'mp', axis=1, tiled=True)]
    pallas_call x0 -> x1, Pallas kernels: none -> 96.4 us  [projected(): pl.pallas_call(functools.partial(project, Y, S, M), out_shape=jax.ShapeDt...]
    ppermute x1, starting transfers between devices: 2.11 us -> 17.4 us  [passed_along(): return lax.ppermute(block, axis, route)]
    dot_general x1 -> x0, matrix products: 9.69 us -> none  [shards(): jnp.einsum('td,pdc->tpc', normed, lax.all_gather(w_in, 'seq', axis=1, til...]
    reduce_sum x1 -> x0, other arithmetic: 5.1 us -> none  [shards(): meansq = jnp.mean(fullf * fullf, axis=1, keepdims=True)]
  transfers between devices with their start and end apart: 3 -> 1, of which waited for: 3 -> 0; matrix products, arithmetic and copies ran while one was open for 3% -> 2% of each run, Pallas kernels for 0% -> 0%
where the time goes in v1:
time: 125 us
  Pallas kernels  96.4 us (77%)
  starting transfers between devices  17.4 us (14%)
  local copies, waits for them, and re-layouts  7.57 us (6%)
  other arithmetic  2.07 us (2%)
  matrix products  1.45 us (1%)
    pallas_call x1, Pallas kernels, projected(): pl.pallas_call(functools.partial(project, Y, S, M), out_shape=jax.ShapeDt...  96.4 us
    ppermute x1, starting transfers between devices, passed_along(): return lax.ppermute(block, axis, route)  17.4 us
  transfers between devices with their start and end apart: 1, of which 0 were waited for; matrix products, arithmetic and copies ran while one was open for 2% of the time, Pallas kernels for 0%

profile of v1, /device:TPU:1, one launch (start us, length us, event | category | flops | bytes accessed | tf_op | source)
XLA Modules:
  0.0 125.1 jit_solution(1879759265843258240)
XLA Ops:
  0.0 96.4 %shard_map.55 = f32[512,384]{1,0:T(8,128)} custom-call(bf16[512,2048]{1,0:T(8,128)(2,1)} %x_ref.1, bf16[3,2048,128]{2,1,0:T(8,128)(2,1)} %w_ref.1), custom_call_target="tpu_custom_call" | custom-call | tf_op jit(solution)/shard_map/pallas_call | solution.py:218
  96.4 1.0 slice.102
  97.4 17.4 %collective-permute-start = (bf16[130,3,128]{2,0,1:T(8,128)(2,1)S(1)}, bf16[130,3,128]{2,0,1:T(8,128)(2,1)}, u32[]{:S(2)}, u32[]{:S(2)}) collective-permute-start(bf16[130,3,128]{2,0,1:T(8,128)(2,1)S(1)} %copy.14), channel_id=1, source_target_pairs={{0,4},{4,8},{8,12},{1,5},{5,9},{9,13},{2,6},{6,10},{10,14},{3,7},{... | collective-permute-start | bytes 299528 | tf_op jit(solution)/shard_map/ppermute | solution.py:17
  114.8 0.0 copy-done.2
  114.8 0.1 rev.3
  114.9 0.1 pad.2.clone
  115.0 0.0 copy-done.3
  115.0 0.1 maximum_maximum_fusion
  115.1 1.4 %copy.15 = f32[512,384]{0,1:T(8,128)S(1)} copy(f32[512,384]{1,0:T(8,128)} %shard_map.55) | data formatting | bytes 1572864 | tf_op jit(solution)/shard_map/pallas_call | solution.py:218
  116.5 0.1 tile.4
  116.6 0.7 tile.10
  117.3 0.0 copy-start
  117.3 0.0 collective-permute-done
  117.3 1.2 copy.16
  118.5 0.9 fusion.4
  119.5 0.9 copy-done.1
  120.5 0.1 concatenate.16
  120.6 0.1 concatenate.15
  120.7 0.0 copy-start.4
  120.8 0.9 slice-done
  121.7 1.5 %convolution_bitcast_fusion = f32[4,128,8,16]{1,3,0,2:T(8,128)S(1)} fusion(f32[1,8,128,256]{3,1,2,0:T(8,128)S(1)} %bitcast.42, f32[4,128,8,16]{1,3,0,2:T(8,128)S(1)} %copy.18, f32[4,128,8,16]{1,3,0,2:T(8,128)S(1)} %copy.17), kind=kOutput, calls=%fused_computation.4 | convolution fusion | flops 201457664 | bytes 1835008 | tf_op jit(solution)/shard_map/gts,bsgk->btgk/dot_general | solution.py:259
  123.1 0.1 copy.19
  123.3 1.0 fusion.12
  124.3 0.8 copy.20
  (17 shorter events, 0.2 us)
Async XLA Ops:
  0.0 114.8 %copy-start.2 = (f32[8,128]{1,0:T(8,128)S(1)}, f32[8,128]{1,0:T(8,128)}, u32[]{:S(2)}) copy-start(f32[8,128]{1,0:T(8,128)} %param.8) | copy-start | bytes 12292
  0.0 115.0 %copy-start.3 = (f32[3,3,128]{2,1,0:T(4,128)S(1)}, f32[3,3,128]{2,1,0:T(4,128)}, u32[]{:S(2)}) copy-start(f32[3,3,128]{2,1,0:T(4,128)} %param.7) | copy-start | bytes 13828
  97.4 19.9 %collective-permute-start = (bf16[130,3,128]{2,0,1:T(8,128)(2,1)S(1)}, bf16[130,3,128]{2,0,1:T(8,128)(2,1)}, u32[]{:S(2)}, u32[]{:S(2)}) collective-permute-start(bf16[130,3,128]{2,0,1:T(8,128)(2,1)S(1)} %copy.14), channel_id=1, source_target_pairs={{0,4},{4,8},{8,12},{1,5},{5,9},{9,13},{2,6},{6,10},{10,14},{3,7},{... | collective-permute-start | bytes 299528 | tf_op jit(solution)/shard_map/ppermute | solution.py:17
  117.3 2.1 %copy-start = (f32[8,32896]{1,0:T(8,128)}, f32[8,32896]{1,0:T(8,128)S(1)}, u32[]{:S(2)}) copy-start(f32[8,32896]{1,0:T(8,128)S(1)} %tile.10) | copy-start | bytes 3158020
  119.4 1.0 copy-start.1
  120.4 1.2 slice-start
  120.7 2.5 %copy-start.4 = (f32[128]{0:T(128)S(1)}, f32[128]{0:T(128)}, u32[]{:S(2)}) copy-start(f32[128]{0:T(128)} %param.9) | copy-start | bytes 1540

commit v2 on v1

--- a/solution.py
+++ b/solution.py
@@ -38,9 +38,9 @@
     def source_is_self(r2):
         return jnp.logical_and(m // R == s, family + S * r2 == m)
 
-    def chunk(y_, x_, core_, r2):
+    def chunk(y_, x_, core_, r2, p):
         c = x_ + core_ * X + S * r2
-        return wbuf.at[c, :, pl.ds(pl.multiple_of(y_ * part_rows, part_rows), part_rows), :]
+        return wbuf.at[c, p, pl.ds(pl.multiple_of(y_ * part_rows, part_rows), part_rows), :]
 
     def arrived(ref, sem):
         pltpu.make_async_copy(ref, ref, sem).wait()
@@ -74,24 +74,24 @@
         peers = peers - is_self(r).astype(jnp.int32) - source_is_self(r).astype(jnp.int32)
     pl.semaphore_wait(barrier, peers)
 
-    def first(r):
+    def first(r, p):
         rows = pl.ds(pl.multiple_of(r * F + y * part_rows, part_rows), part_rows)
-        dst = wbuf.at[m, :, pl.ds(pl.multiple_of(y * part_rows, part_rows), part_rows), :]
-        rx, rc = relay // 2, relay % 2
-        sem = recv_a.at[y, rx, m // S]
-        return w_ref.at[:, rows, :], dst, sem, rx, rc
-
-    for r in range(R):
-        src, dst, sem, _, _ = first(r)
+        dst = wbuf.at[m, p, pl.ds(pl.multiple_of(y * part_rows, part_rows), part_rows), :]
+        rx = relay // 2
+        sem = recv_a.at[y, rx, m // S, p]
+        return w_ref.at[p, rows, :], dst, sem
+
+    for p, r in [(p, r) for p in range(3) for r in range(R)]:
+        src, dst, sem = first(r, p)
 
         @pl.when(is_self(r))
         def _(src=src, dst=dst, sem=sem):
             pltpu.make_async_copy(src, dst, sem).start()
 
         @pl.when(jnp.logical_not(is_self(r)))
-        def _(src=src, dst=dst, sem=sem, r=r):
+        def _(src=src, dst=dst, sem=sem, r=r, p=p):
             pltpu.make_async_remote_copy(
-                src_ref=src, dst_ref=dst, send_sem=send1.at[r], recv_sem=sem,
+                src_ref=src, dst_ref=dst, send_sem=send1.at[r, p], recv_sem=sem,
                 device_id=at(y, relay, R * s + r), device_id_type=pl.DeviceIdType.MESH,
             ).start()
 
@@ -110,51 +110,52 @@
     for k in range(1, M):
         share_squares(k).start()
 
-    def hand(dy, dx, r2):
+    def hand(dy, dx, r2, p):
         yo, xo = other(dy, dx)
-        ref = chunk(y, x, core, r2)
-        return pltpu.make_async_remote_copy(
-            src_ref=ref, dst_ref=ref, send_sem=send_a.at[dy, dx, r2], recv_sem=recv_a.at[y, x, r2],
+        ref = chunk(y, x, core, r2, p)
+        return pltpu.make_async_remote_copy(
+            src_ref=ref, dst_ref=ref, send_sem=send_a.at[dy, dx, r2, p], recv_sem=recv_a.at[y, x, r2, p],
             device_id=at(yo, 2 * xo + core, m), device_id_type=pl.DeviceIdType.MESH)
 
-    def pass_on(dy, dx, r2):
+    def pass_on(dy, dx, r2, p):
         yo, xo = other(dy, dx)
-        ref = chunk(yo, xo, core, r2)
-        return pltpu.make_async_remote_copy(
-            src_ref=ref, dst_ref=ref, send_sem=send_b.at[yo, xo, r2], recv_sem=recv_b.at[yo, xo, r2],
+        ref = chunk(yo, xo, core, r2, p)
+        return pltpu.make_async_remote_copy(
+            src_ref=ref, dst_ref=ref, send_sem=send_b.at[yo, xo, r2, p], recv_sem=recv_b.at[yo, xo, r2, p],
             device_id=at(y, 2 * x + 1 - core, m), device_id_type=pl.DeviceIdType.MESH)
 
-    def send_partial(c):
-        return pltpu.make_async_remote_copy(
-            src_ref=pbuf.at[c], dst_ref=rbuf.at[m], send_sem=send_p.at[c], recv_sem=recv_p.at[m],
+    def send_partial(c, p):
+        return pltpu.make_async_remote_copy(
+            src_ref=pbuf.at[c, p], dst_ref=rbuf.at[m, p], send_sem=send_p.at[c, p],
+            recv_sem=recv_p.at[m, p],
             device_id=at(y, s, c), device_id_type=pl.DeviceIdType.MESH)
 
-    def multiply(c):
-        w = jnp.concatenate([wbuf[c, p] for p in range(3)], axis=1)
-        part = jnp.dot(x_ref[...], w, preferred_element_type=jnp.float32)
+    def multiply(c, p):
+        part = jnp.dot(x_ref[...], wbuf[c, p], preferred_element_type=jnp.float32)
 
         @pl.when(c == m)
         def _():
-            pself[...] = part
+            pself[p] = part
 
         @pl.when(c != m)
         def _():
-            pbuf[c] = part.astype(pbuf.dtype)
-            send_partial(c).start()
-
-    for r2 in range(R):
-        arrived(chunk(y, x, core, r2), recv_a.at[y, x, r2])
-        for dy, dx in others:
-            hand(dy, dx, r2).start()
-        pass_on(0, 0, r2).start()
-
-    def take(dy, dx):
+            pbuf[c, p] = part.astype(pbuf.dtype)
+            send_partial(c, p).start()
+
+    def give(p):
+        for r2 in range(R):
+            arrived(chunk(y, x, core, r2, p), recv_a.at[y, x, r2, p])
+            for dy, dx in others:
+                hand(dy, dx, r2, p).start()
+            pass_on(0, 0, r2, p).start()
+
+    def take(dy, dx, p):
         for r2 in range(R):
             yo, xo = other(dy, dx)
-            arrived(chunk(yo, xo, core, r2), recv_a.at[yo, xo, r2])
-            pass_on(dy, dx, r2).start()
-
-    def work(dx, mine):
+            arrived(chunk(yo, xo, core, r2, p), recv_a.at[yo, xo, r2, p])
+            pass_on(dy, dx, r2, p).start()
+
+    def work(dx, mine, p):
         xo = (x + dx) % X
         core_ = core if mine else 1 - core
 
@@ -162,17 +163,21 @@
             if not mine:
                 for dy in range(Y):
                     yo = (y + dy) % Y
-                    arrived(chunk(yo, xo, core_, r2), recv_b.at[yo, xo, r2])
-            multiply(xo + core_ * X + S * r2)
+                    arrived(chunk(yo, xo, core_, r2, p), recv_b.at[yo, xo, r2, p])
+            multiply(xo + core_ * X + S * r2, p)
             return carry
         lax.fori_loop(0, R, one, 0)
 
-    for dx in range(X):
-        for dy in range(Y):
-            if dy or dx:
-                take(dy, dx)
-        work(dx, True)
-        work(dx, False)
+    give(0)
+    for p in range(3):
+        if p < 2:
+            give(p + 1)
+        for dx in range(X):
+            for dy in range(Y):
+                if dy or dx:
+                    take(dy, dx, p)
+            work(dx, True, p)
+            work(dx, False, p)
 
     for k in range(1, M):
         c = (m + k) % M
@@ -181,32 +186,34 @@
     for c in range(1, M):
         total = total + ssbuf[c]
     inv = lax.rsqrt(total / (F * M) + 1e-06)
-    for k in range(1, M):
-        c = (m + k) % M
-        arrived(rbuf.at[c], recv_p.at[c])
-    for i in range(T // tile):
-        rows = slice(i * tile, (i + 1) * tile)
-
-        def add(k, acc):
-            return acc + rbuf[(m + k) % M, rows, :].astype(jnp.float32)
-        acc = lax.fori_loop(1, M, add, pself[rows, :])
-        scale = jnp.transpose(jnp.broadcast_to(inv[0:1, rows], (128, tile)))
-        out_ref[rows, :] = acc * jnp.concatenate([scale] * 3, axis=1)
-
-    for r in range(R):
-        @pl.when(jnp.logical_not(is_self(r)))
-        def _(r=r):
-            src = first(r)[0]
-            arrived(src, send1.at[r])
+    for p in range(3):
+        for k in range(1, M):
+            c = (m + k) % M
+            arrived(rbuf.at[c, p], recv_p.at[c, p])
+        for i in range(T // tile):
+            rows = slice(i * tile, (i + 1) * tile)
+
+            def add(k, acc):
+                return acc + rbuf[(m + k) % M, p, rows, :].astype(jnp.float32)
+            acc = lax.fori_loop(1, M, add, pself[p, rows, :])
+            scale = jnp.transpose(jnp.broadcast_to(inv[0:1, rows], (128, tile)))
+            out_ref[rows, p * 128:(p + 1) * 128] = acc * scale
+
     for k in range(1, M):
         share_squares(k).wait_send()
-        send_partial((m + k) % M).wait_send()
-    for r2 in range(R):
-        for dy in range(Y):
-            for dx in range(X):
-                if dy or dx:
-                    hand(dy, dx, r2).wait_send()
-                pass_on(dy, dx, r2).wait_send()
+    for p in range(3):
+        for r in range(R):
+            @pl.when(jnp.logical_not(is_self(r)))
+            def _(r=r, p=p):
+                arrived(first(r, p)[0], send1.at[r, p])
+        for k in range(1, M):
+            send_partial((m + k) % M, p).wait_send()
+        for r2 in range(R):
+            for dy in range(Y):
+                for dx in range(X):
+                    if dy or dx:
+                        hand(dy, dx, r2, p).wait_send()
+                    pass_on(dy, dx, r2, p).wait_send()
 
 
 def projected(tokens, w_in):
@@ -222,12 +229,12 @@
         out_specs=pl.BlockSpec(memory_space=pltpu.VMEM),
         scratch_shapes=[
             pltpu.VMEM((M, 3, F, w_in.shape[2]), jnp.bfloat16),
-            pltpu.VMEM((M, T, W), jnp.bfloat16),
-            pltpu.VMEM((M, T, W), jnp.bfloat16),
-            pltpu.VMEM((T, W), jnp.float32),
+            pltpu.VMEM((M, 3, T, W // 3), jnp.bfloat16),
+            pltpu.VMEM((M, 3, T, W // 3), jnp.bfloat16),
+            pltpu.VMEM((3, T, W // 3), jnp.float32),
             pltpu.VMEM((M, 8, T), jnp.float32),
-            dma((R,)), dma((Y, X, R)), dma((Y, X, R)), dma((Y, X, R)), dma((Y, X, R)),
-            dma((M,)), dma((M,)), dma((M,)), dma((M,)),
+            dma((R, 3)), dma((Y, X, R, 3)), dma((Y, X, R, 3)), dma((Y, X, R, 3)), dma((Y, X, R, 3)),
+            dma((M, 3)), dma((M, 3)), dma((M,)), dma((M,)),
         ],
         compiler_params=pltpu.CompilerParams(
             collective_id=0, has_side_effects=True, vmem_limit_bytes=56 * 2**20),

time: 125 us -> 95.2 us (0.76)
  Pallas kernels: 96.4 us -> 75.5 us
  starting transfers between devices: 17.4 us -> 8.07 us
    pallas_call x1, Pallas kernels: 96.4 us -> 75.5 us  [projected(): pl.pallas_call(functools.partial(project, Y, S, M), out_shape=jax.ShapeDt...]
    ppermute x1, starting transfers between devices: 17.4 us -> 8.07 us  [passed_along(): return lax.ppermute(block, axis, route)]
  transfers between devices with their start and end apart: 1 -> 1, of which waited for: 0 -> 0; matrix products, arithmetic and copies ran while one was open for 2% -> 3% of each run, Pallas kernels for 0% -> 0%
where the time goes in v2:
time: 95.2 us; the launch traced here: 94.9 us
  Pallas kernels  75.5 us (79%)
  starting transfers between devices  8.07 us (8%)
  local copies, waits for them, and re-layouts  7.57 us (8%)
  other arithmetic  2.07 us (2%)
  matrix products  1.45 us (2%)
    pallas_call x1, Pallas kernels, projected(): pl.pallas_call(functools.partial(project, Y, S, M), out_shape=jax.ShapeDt...  75.5 us
    ppermute x1, starting transfers between devices, passed_along(): return lax.ppermute(block, axis, route)  8.07 us
  transfers between devices with their start and end apart: 1, of which 0 were waited for; matrix products, arithmetic and copies ran while one was open for 3% of the time, Pallas kernels for 0%

profile of v2, /device:TPU:1, one launch (start us, length us, event | category | flops | bytes accessed | tf_op | source)
XLA Modules:
  0.0 94.9 jit_solution(14840398300377928503)
XLA Ops:
  0.0 75.5 %shard_map.55 = f32[512,384]{1,0:T(8,128)} custom-call(bf16[512,2048]{1,0:T(8,128)(2,1)} %x_ref.1, bf16[3,2048,128]{2,1,0:T(8,128)(2,1)} %w_ref.1), custom_call_target="tpu_custom_call" | custom-call | tf_op jit(solution)/shard_map/pallas_call | solution.py:225
  75.5 1.0 %slice.102 = bf16[130,384]{1,0:T(8,128)(2,1)S(1)} slice(f32[512,384]{1,0:T(8,128)} %shard_map.55), slice={[382:512], [0:384]} | slice | bytes 199680 | tf_op jit(solution)/shard_map/slice | solution.py:250
  76.5 8.1 %collective-permute-start = (bf16[130,3,128]{2,0,1:T(8,128)(2,1)S(1)}, bf16[130,3,128]{2,0,1:T(8,128)(2,1)}, u32[]{:S(2)}, u32[]{:S(2)}) collective-permute-start(bf16[130,3,128]{2,0,1:T(8,128)(2,1)S(1)} %copy.14), channel_id=1, source_target_pairs={{0,4},{4,8},{8,12},{1,5},{5,9},{9,13},{2,6},{6,10},{10,14},{3,7},{... | collective-permute-start | bytes 299528 | tf_op jit(solution)/shard_map/ppermute | solution.py:17
  84.6 0.0 copy-done.2
  84.6 0.1 rev.3
  84.7 0.1 pad.2.clone
  84.8 0.0 copy-done.3
  84.8 0.1 maximum_maximum_fusion
  84.9 1.4 %copy.15 = f32[512,384]{0,1:T(8,128)S(1)} copy(f32[512,384]{1,0:T(8,128)} %shard_map.55) | data formatting | bytes 1572864 | tf_op jit(solution)/shard_map/pallas_call | solution.py:225
  86.3 0.1 tile.4
  86.4 0.7 tile.10
  87.1 0.0 copy-start
  87.1 0.0 collective-permute-done
  87.1 1.2 %copy.16 = f32[130,3,128]{0,2,1:T(8,128)S(1)} copy(bf16[130,3,128]{2,0,1:T(8,128)(2,1)} %collective-permute-done) | data formatting | bytes 299520 | tf_op jit(solution)/shard_map/convert_element_type | solution.py:250
  88.3 0.9 fusion.4
  89.3 0.9 copy-done.1
  90.3 0.1 concatenate.16
  90.4 0.1 concatenate.15
  90.5 0.0 copy-start.4
  90.6 0.9 slice-done
  91.5 1.5 %convolution_bitcast_fusion = f32[4,128,8,16]{1,3,0,2:T(8,128)S(1)} fusion(f32[1,8,128,256]{3,1,2,0:T(8,128)S(1)} %bitcast.42, f32[4,128,8,16]{1,3,0,2:T(8,128)S(1)} %copy.18, f32[4,128,8,16]{1,3,0,2:T(8,128)S(1)} %copy.17), kind=kOutput, calls=%fused_computation.4 | convolution fusion | flops 201457664 | bytes 1835008 | tf_op jit(solution)/shard_map/gts,bsgk->btgk/dot_general | solution.py:266
  92.9 0.1 copy.19
  93.1 1.0 %fusion.12 = bf16[512,128]{0,1:T(8,128)(2,1)S(1)} fusion(f32[16,8,4,128]{3,2,1,0:T(4,128)S(1)} %bitcast.44, f32[640,3,128]{0,2,1:T(8,128)} %copy-done.1, f32[128]{0:T(128)S(1)} %copy-done.4, f32[640,1,128]{0,2,1:T(8,128)S(1)} %slice_multiply_fusion), kind=kLoop, calls=%fused_computation.21 | loop fusion | flops 262144 | bytes 918016 | tf_op jit(solution)/shard_map/convert_element_type | solution.py:268
  94.1 0.8 copy.20
  (17 shorter events, 0.2 us)
Async XLA Ops:
  0.0 84.6 %copy-start.2 = (f32[8,128]{1,0:T(8,128)S(1)}, f32[8,128]{1,0:T(8,128)}, u32[]{:S(2)}) copy-start(f32[8,128]{1,0:T(8,128)} %param.8) | copy-start | bytes 12292
  0.0 84.8 %copy-start.3 = (f32[3,3,128]{2,1,0:T(4,128)S(1)}, f32[3,3,128]{2,1,0:T(4,128)}, u32[]{:S(2)}) copy-start(f32[3,3,128]{2,1,0:T(4,128)} %param.7) | copy-start | bytes 13828
  76.5 10.6 %collective-permute-start = (bf16[130,3,128]{2,0,1:T(8,128)(2,1)S(1)}, bf16[130,3,128]{2,0,1:T(8,128)(2,1)}, u32[]{:S(2)}, u32[]{:S(2)}) collective-permute-start(bf16[130,3,128]{2,0,1:T(8,128)(2,1)S(1)} %copy.14), channel_id=1, source_target_pairs={{0,4},{4,8},{8,12},{1,5},{5,9},{9,13},{2,6},{6,10},{10,14},{3,7},{... | collective-permute-start | bytes 299528 | tf_op jit(solution)/shard_map/ppermute | solution.py:17
  87.1 2.1 %copy-start = (f32[8,32896]{1,0:T(8,128)}, f32[8,32896]{1,0:T(8,128)S(1)}, u32[]{:S(2)}) copy-start(f32[8,32896]{1,0:T(8,128)S(1)} %tile.10) | copy-start | bytes 3158020
  89.2 1.0 %copy-start.1 = (f32[640,3,128]{0,2,1:T(8,128)}, f32[640,3,128]{0,2,1:T(8,128)S(1)}, u32[]{:S(2)}) copy-start(f32[640,3,128]{0,2,1:T(8,128)S(1)} %fusion.4) | copy-start | bytes 2949124
  90.2 1.2 %slice-start = ((f32[8,32896]{1,0:T(8,128)}), f32[8,32768]{1,0:T(8,128)S(1)}, s32[]{:S(2)}) async-start(f32[8,32896]{1,0:T(8,128)} %copy-done), calls=%async_computation | async-start | bytes 2097152 | tf_op jit(solution)/shard_map/slice | solution.py:265
  90.5 2.5 %copy-start.4 = (f32[128]{0:T(128)S(1)}, f32[128]{0:T(128)}, u32[]{:S(2)}) copy-start(f32[128]{0:T(128)} %param.9) | copy-start | bytes 1540
